TPU v7x, 32 devices: a whole 2x2x4 slice. The times are simulated.
32 devices in a mesh: gx: 8 (over y, x, core), pa: 4 (over z).
Axes of the slice: x: 2, y: 2, z: 4, core: 2. Of those that a mesh axis runs over, the one named last changes fastest.
Arguments:
- block_inverses: float32 [32, 32, 128, 128], P('gx', 'pa'), parts along dimension 1, may hold values from -0.25 to 1.07, as said below
- residual: float32 [32, 32, 128], P('gx', 'pa'), parts along dimension 1, may hold values from -0.3 to 0.3
- material: int32 [32, 32, 128], P('gx', 'pa'), parts along dimension 1, may hold values from 0 to 3
- fin_mask: int32 [32, 32, 128], P('gx', 'pa'), parts along dimension 1, may hold values 0 or 1
- phase_mask: int32 [32, 32, 128], P('gx', 'pa'), parts along dimension 1, may hold values 0 or 1
- k_table: float32 [4], replicated, may hold values from 0.95 to 1.05
Outputs:
- correction: float32 [32, 32, 128], P('gx', 'pa'), parts along dimension 1
- enthalpy_step: float32 [32, 32, 128], P('gx', 'pa'), parts along dimension 1
There are 4 independent parts, one for each index of `pa`. A program takes and returns all parts, laid end to end along the dimension named above; an argument that names none is the same for every part. Nothing has to cross between parts.
Inputs may be any that keep to these rules, and one draw needn't show every extreme that they name: Each block block_inverses[i, t] is a symmetric matrix.
All inputs are finite; a program needn't handle non-finite values. No bound on the sum of `fin_mask` or of `phase_mask` on one device may be relied on, other than what follows from the above.
Results may differ from a plain program's by a relative error of at most 0.0003.
Values sent between devices are 32-bit elements; how exact they have to be, the bound alone decides.
No kernel may reach another device: no remote copies, remote signals or barrier semaphores. Data moves between devices by JAX's collectives and lax.ppermute only.
A program may use at most 128 MiB of HBM per device.

v0:
```python
import jax
import jax.numpy as jnp
from jax import lax
from jax.sharding import PartitionSpec as P


def passed_along(block, axis, distance):
    devices = range(lax.axis_size(axis))
    route = [(i - distance, i) for i in devices if i - distance in devices]
    return lax.ppermute(block, axis, route)


def apply_block(pivot_entries, vector):
    return jnp.einsum("tab,tb->ta", pivot_entries, vector, precision=lax.Precision.HIGHEST)


def apply_transposed(pivot_entries, vector):
    return jnp.einsum("tba,tb->ta", pivot_entries, vector, precision=lax.Precision.HIGHEST)


def forward_pass(block_inverses, residual, face_cond, entering):
    state_vec = entering
    results = []
    for line_position in range(block_inverses.shape[0]):
        state_vec = apply_block(
            block_inverses[line_position],
            residual[line_position] + face_cond[line_position] * state_vec,
        )
        results.append(state_vec)
    return jnp.stack(results)


def backward_pass(block_inverses, forward_vals, face_cond, arriving):
    carried = arriving
    results = [None] * block_inverses.shape[0]
    for line_position in reversed(range(block_inverses.shape[0])):
        solved = forward_vals[line_position] + apply_block(block_inverses[line_position], carried)
        results[line_position] = solved
        carried = face_cond[line_position] * solved
    return (jnp.stack(results), carried)


def on_device(block_inverses, residual, material, fin_mask, phase_mask, k_table):
    block_count, tile_count, cell_count = residual.shape
    material_codes = jnp.arange(k_table.shape[0], dtype=jnp.int32)
    conduct = jnp.sum(
        jnp.where(material[..., None] == material_codes, k_table, jnp.zeros_like(k_table)), axis=-1
    )
    before = passed_along(conduct[block_count - 1], "gx", 1)
    earlier = jnp.concatenate([before[None], conduct[: block_count - 1]], axis=0)
    face_cond = (
        2.0 * conduct * earlier / (conduct + earlier) * (0.9 + 0.1 * fin_mask.astype(jnp.float32))
    )
    zero_vector = jnp.zeros((tile_count, cell_count), jnp.float32)
    scaled_rows = block_inverses * face_cond[:, :, None, :]
    matrix_product = scaled_rows[0]
    for line_position in range(1, block_count):
        matrix_product = jnp.einsum(
            "hzp,hpn->hzn",
            scaled_rows[line_position],
            matrix_product,
            precision=lax.Precision.HIGHEST,
        )
    local_vals = forward_pass(block_inverses, residual, face_cond, zero_vector)
    tail_vec = local_vals[block_count - 1]
    all_maps, all_tails = (
        lax.all_gather(matrix_product[None], "gx", axis=0, tiled=True),
        lax.all_gather(tail_vec[None], "gx", axis=0, tiled=True),
    )
    own_index = lax.axis_index("gx")
    processor_total = all_maps.shape[0]

    def fold_forward(line_position, state_vec):
        moved = apply_block(all_maps[line_position], state_vec) + all_tails[line_position]
        return jnp.where(line_position < own_index, moved, state_vec)

    entering = lax.fori_loop(0, processor_total, fold_forward, zero_vector, unroll=8)
    forward_vals = forward_pass(block_inverses, residual, face_cond, entering)
    _, leaving = backward_pass(block_inverses, forward_vals, face_cond, zero_vector)
    all_leaving = lax.all_gather(leaving[None], "gx", axis=0, tiled=True)

    def backward_accumulate(offset, state_vec):
        line_position = processor_total - 1 - offset
        moved = apply_transposed(all_maps[line_position], state_vec) + all_leaving[line_position]
        return jnp.where(line_position > own_index, moved, state_vec)

    arriving = lax.fori_loop(0, processor_total, backward_accumulate, zero_vector, unroll=8)
    correction, _ = backward_pass(block_inverses, forward_vals, face_cond, arriving)
    enthalpy_step = correction * (1.0 + 2.0 * phase_mask.astype(jnp.float32))
    return (correction, enthalpy_step)


def solution(mesh):
    return jax.shard_map(
        on_device,
        mesh=mesh,
        in_specs=(
            P("gx", "pa", None, None),
            P("gx", "pa", None),
            P("gx", "pa", None),
            P("gx", "pa", None),
            P("gx", "pa", None),
            P(),
        ),
        out_specs=(P("gx", "pa", None), P("gx", "pa", None)),
        check_vma=False,
    )
```

profile of v0, /device:TPU:0, one launch (start us, length us, event | category | flops | bytes accessed | tf_op | source)
XLA Modules:
  0.0 100.5 jit_solution(474527091113292094)
XLA Ops:
  7.2 0.8 select_reduce_fusion
  8.0 2.3 %collective-permute-start = (f32[8,128]{1,0:T(8,128)S(1)}, f32[8,128]{1,0:T(8,128)S(1)}, u32[]{:S(2)}, u32[]{:S(2)}) collective-permute-start(f32[8,128]{1,0:T(8,128)S(1)} %slice_bitcast_fusion.12), channel_id=1, source_target_pairs={{0,4},{4,8},{8,12},{12,16},{16,20},{20,24},{24,28},{1,5},{5,9},{9,... | collective-permute-start | bytes 12296 | tf_op jit(solution)/shard_map/ppermute | solution.py:10
  10.4 0.8 collective-permute-done
  11.9 1.9 %broadcast_multiply_fusion = f32[4,8,128,128]{3,2,1,0:T(8,128)S(1)} fusion(f32[4,8,128,128]{3,2,1,0:T(8,128)} %param.6, f32[4,8,128]{2,1,0:T(8,128)S(1)} %add_multiply_fusion.1), kind=kLoop, calls=%fused_computation | loop fusion | flops 524288 | bytes 4210688 | tf_op jit(solution)/shard_map/mul | solution.py:55
  15.2 1.5 %fusion.2 = f32[8,128,128]{2,1,0:T(8,128)} fusion(f32[8,128,128]{2,1,0:T(8,128)S(1)} %fusion.1, f32[4,8,128,128]{3,2,1,0:T(8,128)S(1)} %broadcast_multiply_fusion), kind=kOutput, calls=%fused_computation.7 | convolution fusion | flops 201326592 | bytes 1572864 | tf_op jit(solution)/shard_map/hzp,hpn->hzn/dot_general | solution.py:58
  16.8 0.9 fusion.5
  17.7 0.9 fusion.33
  18.6 0.9 fusion.25
  19.6 1.0 fusion.17
  20.5 0.9 fusion.9
  21.5 13.4 %all-gather.1 = f32[64,128]{1,0:T(8,128)S(1)} all-gather(f32[8,128]{1,0:T(8,128)S(1)} %bitcast.349), channel_id=3, replica_groups=mesh['gx'=8,'pa'=4] {'gx'}, dimensions={0}, use_global_device_ids=true | all-gather | bytes 36864 | tf_op jit(solution)/shard_map/all_gather | solution.py:68
  34.8 23.2 %all-gather.5.cloned.1.call-done = f32[64,128,128]{2,1,0:T(8,128)} async-done(((f32[8,128,128]{2,1,0:T(8,128)}), f32[64,128,128]{2,1,0:T(8,128)}) %all-gather.5.cloned.1.call-update) | async-done | bytes 4194320 | tf_op jit(solution)/shard_map/all_gather | solution.py:67
  58.0 2.1 %fusion.72 = f32[8,1,128]{2,1,0:T(1,128)S(1)} fusion(f32[64,128,128]{2,1,0:T(8,128)} %all-gather.5.cloned.1.call-done, f32[8,128,1]{1,2,0:T(1,128)S(1)} %bitcast.312), kind=kOutput, calls=%fused_computation.119 | convolution fusion | flops 1572864 | bytes 4202496 | tf_op jit(solution)/shard_map/eval_jaxpr/tab,tb->ta/dot_general | solution.py:14
  60.1 2.0 %fusion.73 = f32[8,1,128]{2,1,0:T(1,128)S(1)} fusion(f32[64,128,128]{2,1,0:T(8,128)} %all-gather.5.cloned.1.call-done, f32[8,128,1]{1,2,0:T(1,128)S(1)} %bitcast.326), kind=kOutput, calls=%fused_computation.120 | convolution fusion | flops 1572864 | bytes 4202496 | tf_op jit(solution)/shard_map/eval_jaxpr/tab,tb->ta/dot_general | solution.py:14
  62.1 2.0 %fusion.74 = f32[8,1,128]{2,1,0:T(1,128)S(1)} fusion(f32[64,128,128]{2,1,0:T(8,128)} %all-gather.5.cloned.1.call-done, f32[8,128,1]{1,2,0:T(1,128)S(1)} %bitcast.329), kind=kOutput, calls=%fused_computation.121 | convolution fusion | flops 1572864 | bytes 4202496 | tf_op jit(solution)/shard_map/eval_jaxpr/tab,tb->ta/dot_general | solution.py:14
  64.1 0.9 fusion.75
  65.0 0.9 fusion.76
  66.0 0.9 fusion.77
  66.9 0.9 fusion.78
  67.9 0.9 fusion.79
  68.8 0.9 fusion.31
  69.7 0.9 fusion.23
  70.7 0.9 fusion.15
  71.6 0.9 fusion.7
  72.6 0.9 fusion.13
  73.5 0.9 fusion.21
  74.5 0.9 fusion.29
  75.4 9.2 %all-gather.2 = f32[64,128]{1,0:T(8,128)S(1)} all-gather(f32[8,128]{1,0:T(8,128)S(1)} %add_multiply_fusion.2), channel_id=4, replica_groups=mesh['gx'=8,'pa'=4] {'gx'}, dimensions={0}, use_global_device_ids=true | all-gather | bytes 36864 | tf_op jit(solution)/shard_map/all_gather | solution.py:80
  89.2 0.9 fusion.3
  90.2 0.9 fusion.11
  91.1 0.9 fusion.19
  92.0 0.9 fusion.27
  (56 shorter events, 7.5 us)
Async XLA Ops:
  7.2 50.9 %all-gather.5.cloned.1.call-start = ((), (), s32[]{:S(2)}) async-start(), calls=%async_computation | async-start | bytes 4718592 | tf_op jit(solution)/shard_map/all_gather | solution.py:67
  8.0 3.2 %collective-permute-start = (f32[8,128]{1,0:T(8,128)S(1)}, f32[8,128]{1,0:T(8,128)S(1)}, u32[]{:S(2)}, u32[]{:S(2)}) collective-permute-start(f32[8,128]{1,0:T(8,128)S(1)} %slice_bitcast_fusion.12), channel_id=1, source_target_pairs={{0,4},{4,8},{8,12},{12,16},{16,20},{20,24},{24,28},{1,5},{5,9},{9,... | collective-permute-start | bytes 12296 | tf_op jit(solution)/shard_map/ppermute | solution.py:10
  11.9 4.8 %copy-start.1 = (f32[4,8,128,128]{3,2,1,0:T(8,128)S(1)}, f32[4,8,128,128]{3,2,1,0:T(8,128)}, u32[]{:S(2)}) copy-start(f32[4,8,128,128]{3,2,1,0:T(8,128)} %param.6) | copy-start | bytes 6291460
  11.9 5.8 %copy-start.2 = (f32[4,8,128]{2,1,0:T(8,128)S(1)}, f32[4,8,128]{2,1,0:T(8,128)}, u32[]{:S(2)}) copy-start(f32[4,8,128]{2,1,0:T(8,128)} %param.7) | copy-start | bytes 49156
  58.0 6.1 %copy-start = (f32[64,128,128]{2,1,0:T(8,128)S(1)}, f32[64,128,128]{2,1,0:T(8,128)}, u32[]{:S(2)}) copy-start(f32[64,128,128]{2,1,0:T(8,128)} %all-gather.5.cloned.1.call-done) | copy-start | bytes 12582916
  86.9 6.1 %copy-start.3 = (s32[4,8,128]{2,1,0:T(8,128)S(1)}, s32[4,8,128]{2,1,0:T(8,128)}, u32[]{:S(2)}) copy-start(s32[4,8,128]{2,1,0:T(8,128)} %param.10) | copy-start | bytes 49156
Sparse Core Ops, SparseCore 0:
  16.8 41.1 all-gather.4
where the time goes:
time: 101 us; the launch traced here: 100 us
  matrix products  32.9 us (33%)
  waiting for transfers between devices  24 us (24%)
  blocking collectives  22.6 us (22%)
  between operations  14.2 us (14%)
  other arithmetic  4.31 us (4%)
  starting transfers between devices  2.38 us (2%)
    dot_general x24, matrix products, apply_block(): jnp.einsum('tab,tb->ta', pivot_entries, vector, precision=lax.Precision.H...  25.7 us
    all_gather x1, waiting for transfers between devices, on_device(): lax.all_gather(matrix_product[None], 'gx', axis=0, tiled=True)  23.2 us
    all_gather x1, blocking collectives, on_device(): lax.all_gather(tail_vec[None], 'gx', axis=0, tiled=True)  13.4 us
    all_gather x1, blocking collectives, on_device(): all_leaving = lax.all_gather(leaving[None], 'gx', axis=0, tiled=True)  9.25 us
    dot_general x8, matrix products, apply_transposed(): jnp.einsum('tba,tb->ta', pivot_entries, vector, precision=lax.Precision.H...  4.48 us
    dot_general x3, matrix products, on_device(): jnp.einsum('hzp,hpn->hzn', scaled_rows[line_position], matrix_product, pr...  2.81 us
    ppermute x1, starting transfers between devices, passed_along(): return lax.ppermute(block, axis, route)  2.35 us
  transfers between devices with their start and end apart: 2, of which 2 were waited for; matrix products, arithmetic and copies ran while one was open for 5% of the time, Pallas kernels for 0%

commit v1 on v0

--- a/solution.py
+++ b/solution.py
@@ -77,7 +77,12 @@
     entering = lax.fori_loop(0, processor_total, fold_forward, zero_vector, unroll=8)
     forward_vals = forward_pass(block_inverses, residual, face_cond, entering)
     _, leaving = backward_pass(block_inverses, forward_vals, face_cond, zero_vector)
-    all_leaving = lax.all_gather(leaving[None], "gx", axis=0, tiled=True)
+    ring = [leaving[None]]
+    for hop in range(7):
+        ring.append(lax.ppermute(ring[-1], "gx", [(dev, (dev + 1) % 8) for dev in range(8)]))
+    all_leaving = jnp.roll(
+        jnp.concatenate(ring[::-1], axis=0), (lax.axis_index("gx") + 1) * ring[0].shape[0], axis=0
+    )
 
     def backward_accumulate(offset, state_vec):
         line_position = processor_total - 1 - offset

time: 101 us -> 121 us (1.20)
  waiting for transfers between devices: 24 us -> 49.7 us
  blocking collectives: 22.6 us -> 13.4 us
  matrix products: 32.9 us -> 36 us
    ppermute x0 -> x7, waiting for transfers between devices: none -> 25.7 us  [on_device(): lax.ppermute(ring[-1], 'gx', [(dev, (dev + 1) % 8) for dev in range(8)])]
    all_gather x1 -> x0, blocking collectives: 9.25 us -> none  [on_device(): all_leaving = lax.all_gather(leaving[None], 'gx', axis=0, tiled=True)]
    dot_general x8, matrix products: 4.48 us -> 7.57 us  [apply_transposed(): jnp.einsum('tba,tb->ta', pivot_entries, vector, precision=lax.Precision.H...]
  transfers between devices with their start and end apart: 2 -> 9, of which waited for: 2 -> 9; matrix products, arithmetic and copies ran while one was open for 5% -> 5% of each run, Pallas kernels for 0% -> 0%
where the time goes in v1:
time: 121 us; the launch traced here: 120 us
  waiting for transfers between devices  49.7 us (41%)
  matrix products  36 us (30%)
  between operations  14.3 us (12%)
  blocking collectives  13.4 us (11%)
  other arithmetic  4.33 us (4%)
  starting transfers between devices  2.69 us (2%)
    dot_general x24, matrix products, apply_block(): jnp.einsum('tab,tb->ta', pivot_entries, vector, precision=lax.Precision.H...  25.7 us
    ppermute x7, waiting for transfers between devices, on_device(): lax.ppermute(ring[-1], 'gx', [(dev, (dev + 1) % 8) for dev in range(8)])  25.7 us
    all_gather x1, waiting for transfers between devices, on_device(): lax.all_gather(matrix_product[None], 'gx', axis=0, tiled=True)  23.2 us
    all_gather x1, blocking collectives, on_device(): lax.all_gather(tail_vec[None], 'gx', axis=0, tiled=True)  13.4 us
    dot_general x8, matrix products, apply_transposed(): jnp.einsum('tba,tb->ta', pivot_entries, vector, precision=lax.Precision.H...  7.57 us
    dot_general x3, matrix products, on_device(): jnp.einsum('hzp,hpn->hzn', scaled_rows[line_position], matrix_product, pr...  2.79 us
  transfers between devices with their start and end apart: 9, of which 9 were waited for; matrix products, arithmetic and copies ran while one was open for 5% of the time, Pallas kernels for 0%

profile of v1, /device:TPU:0, one launch (start us, length us, event | category | flops | bytes accessed | tf_op | source)
XLA Modules:
  0.0 120.5 jit_solution(5838484401026664042)
XLA Ops:
  8.0 2.3 %collective-permute-start = (f32[8,128]{1,0:T(8,128)S(1)}, f32[8,128]{1,0:T(8,128)S(1)}, u32[]{:S(2)}, u32[]{:S(2)}) collective-permute-start(f32[8,128]{1,0:T(8,128)S(1)} %slice_bitcast_fusion.12), channel_id=1, source_target_pairs={{0,4},{4,8},{8,12},{12,16},{16,20},{20,24},{24,28},{1,5},{5,9},{9,... | collective-permute-start | bytes 12296 | tf_op jit(solution)/shard_map/ppermute | solution.py:10
  11.9 1.9 %broadcast_multiply_fusion = f32[4,8,128,128]{3,2,1,0:T(8,128)S(1)} fusion(f32[4,8,128,128]{3,2,1,0:T(8,128)} %param.6, f32[4,8,128]{2,1,0:T(8,128)S(1)} %add_multiply_fusion.1), kind=kLoop, calls=%fused_computation | loop fusion | flops 524288 | bytes 4210688 | tf_op jit(solution)/shard_map/mul | solution.py:55
  15.2 1.5 %fusion.2 = f32[8,128,128]{2,1,0:T(8,128)} fusion(f32[8,128,128]{2,1,0:T(8,128)S(1)} %fusion.1, f32[4,8,128,128]{3,2,1,0:T(8,128)S(1)} %broadcast_multiply_fusion), kind=kOutput, calls=%fused_computation.7 | convolution fusion | flops 201326592 | bytes 1572864 | tf_op jit(solution)/shard_map/hzp,hpn->hzn/dot_general | solution.py:58
  17.7 0.9 fusion.33
  18.6 0.9 fusion.25
  19.6 1.0 fusion.17
  21.4 13.4 %all-gather.1 = f32[64,128]{1,0:T(8,128)S(1)} all-gather(f32[8,128]{1,0:T(8,128)S(1)} %bitcast.406), channel_id=3, replica_groups=mesh['gx'=8,'pa'=4] {'gx'}, dimensions={0}, use_global_device_ids=true | all-gather | bytes 36864 | tf_op jit(solution)/shard_map/all_gather | solution.py:68
  34.8 23.2 %all-gather.4.cloned.1.call-done = f32[64,128,128]{2,1,0:T(8,128)} async-done(((f32[8,128,128]{2,1,0:T(8,128)}), f32[64,128,128]{2,1,0:T(8,128)}) %all-gather.4.cloned.1.call-update) | async-done | bytes 4194320 | tf_op jit(solution)/shard_map/all_gather | solution.py:67
  58.0 2.1 %fusion.80 = f32[8,1,128]{2,1,0:T(1,128)S(1)} fusion(f32[64,128,128]{2,1,0:T(8,128)} %all-gather.4.cloned.1.call-done, f32[8,128,1]{1,2,0:T(1,128)S(1)} %bitcast.362), kind=kOutput, calls=%fused_computation.143 | convolution fusion | flops 1572864 | bytes 4202496 | tf_op jit(solution)/shard_map/eval_jaxpr/tab,tb->ta/dot_general | solution.py:14
  60.1 2.0 %fusion.81 = f32[8,1,128]{2,1,0:T(1,128)S(1)} fusion(f32[64,128,128]{2,1,0:T(8,128)} %all-gather.4.cloned.1.call-done, f32[8,128,1]{1,2,0:T(1,128)S(1)} %bitcast.383), kind=kOutput, calls=%fused_computation.144 | convolution fusion | flops 1572864 | bytes 4202496 | tf_op jit(solution)/shard_map/eval_jaxpr/tab,tb->ta/dot_general | solution.py:14
  62.1 2.0 %fusion.82 = f32[8,1,128]{2,1,0:T(1,128)S(1)} fusion(f32[64,128,128]{2,1,0:T(8,128)} %all-gather.4.cloned.1.call-done, f32[8,128,1]{1,2,0:T(1,128)S(1)} %bitcast.384), kind=kOutput, calls=%fused_computation.145 | convolution fusion | flops 1572864 | bytes 4202496 | tf_op jit(solution)/shard_map/eval_jaxpr/tab,tb->ta/dot_general | solution.py:14
  68.8 0.9 fusion.31
  69.7 0.9 fusion.23
  70.7 0.9 fusion.15
  71.6 0.9 fusion.7
  72.6 0.9 fusion.13
  73.5 0.9 fusion.21
  74.5 0.9 fusion.29
  75.7 3.7 %collective-permute-done.1 = f32[1,8,128]{2,1,0:T(8,128)S(1)} collective-permute-done((f32[1,8,128]{2,1,0:T(8,128)S(1)}, f32[1,8,128]{2,1,0:T(8,128)S(1)}, u32[]{:S(2)}, u32[]{:S(2)}) %collective-permute-start.1) | collective-permute-done | bytes 4128 | tf_op jit(solution)/shard_map/ppermute | solution.py:82
  79.4 3.9 %collective-permute-done.2 = f32[1,8,128]{2,1,0:T(8,128)S(1)} collective-permute-done((f32[1,8,128]{2,1,0:T(8,128)S(1)}, f32[1,8,128]{2,1,0:T(8,128)S(1)}, u32[]{:S(2)}, u32[]{:S(2)}) %collective-permute-start.2) | collective-permute-done | bytes 4128 | tf_op jit(solution)/shard_map/ppermute | solution.py:82
  83.3 3.9 %collective-permute-done.3 = f32[1,8,128]{2,1,0:T(8,128)S(1)} collective-permute-done((f32[1,8,128]{2,1,0:T(8,128)S(1)}, f32[1,8,128]{2,1,0:T(8,128)S(1)}, u32[]{:S(2)}, u32[]{:S(2)}) %collective-permute-start.3) | collective-permute-done | bytes 4128 | tf_op jit(solution)/shard_map/ppermute | solution.py:82
  87.2 3.9 %collective-permute-done.4 = f32[1,8,128]{2,1,0:T(8,128)S(1)} collective-permute-done((f32[1,8,128]{2,1,0:T(8,128)S(1)}, f32[1,8,128]{2,1,0:T(8,128)S(1)}, u32[]{:S(2)}, u32[]{:S(2)}) %collective-permute-start.4) | collective-permute-done | bytes 4128 | tf_op jit(solution)/shard_map/ppermute | solution.py:82
  91.2 3.9 %collective-permute-done.5 = f32[1,8,128]{2,1,0:T(8,128)S(1)} collective-permute-done((f32[1,8,128]{2,1,0:T(8,128)S(1)}, f32[1,8,128]{2,1,0:T(8,128)S(1)}, u32[]{:S(2)}, u32[]{:S(2)}) %collective-permute-start.5) | collective-permute-done | bytes 4128 | tf_op jit(solution)/shard_map/ppermute | solution.py:82
  95.1 3.9 %collective-permute-done.6 = f32[1,8,128]{2,1,0:T(8,128)S(1)} collective-permute-done((f32[1,8,128]{2,1,0:T(8,128)S(1)}, f32[1,8,128]{2,1,0:T(8,128)S(1)}, u32[]{:S(2)}, u32[]{:S(2)}) %collective-permute-start.6) | collective-permute-done | bytes 4128 | tf_op jit(solution)/shard_map/ppermute | solution.py:82
  99.0 1.6 %fusion.88 = f32[8,1,128]{2,1,0:T(1,128)S(1)} fusion(f32[64,128,128]{2,1,0:T(8,128)} %all-gather.4.cloned.1.call-done, f32[8,128,1]{1,2,0:T(1,128)S(1)} %bitcast.363), kind=kOutput, calls=%fused_computation.151 | convolution fusion | flops 1572864 | bytes 4202496 | tf_op jit(solution)/shard_map/eval_jaxpr/tba,tb->ta/dot_general | solution.py:18
  100.6 2.3 %collective-permute-done.7 = f32[1,8,128]{2,1,0:T(8,128)S(1)} collective-permute-done((f32[1,8,128]{2,1,0:T(8,128)S(1)}, f32[1,8,128]{2,1,0:T(8,128)S(1)}, u32[]{:S(2)}, u32[]{:S(2)}) %collective-permute-start.7) | collective-permute-done | bytes 4128 | tf_op jit(solution)/shard_map/ppermute | solution.py:82
  103.1 1.6 %fusion.89 = f32[8,1,128]{2,1,0:T(1,128)S(1)} fusion(f32[64,128,128]{2,1,0:T(8,128)} %all-gather.4.cloned.1.call-done, f32[8,128,1]{1,2,0:T(1,128)S(1)} %bitcast.379), kind=kOutput, calls=%fused_computation.152 | convolution fusion | flops 1572864 | bytes 4202496 | tf_op jit(solution)/shard_map/eval_jaxpr/tba,tb->ta/dot_general | solution.py:18
  104.7 1.6 %fusion.90 = f32[8,1,128]{2,1,0:T(1,128)S(1)} fusion(f32[64,128,128]{2,1,0:T(8,128)} %all-gather.4.cloned.1.call-done, f32[8,128,1]{1,2,0:T(1,128)S(1)} %bitcast.374), kind=kOutput, calls=%fused_computation.153 | convolution fusion | flops 1572864 | bytes 4202496 | tf_op jit(solution)/shard_map/eval_jaxpr/tba,tb->ta/dot_general | solution.py:18
  109.2 0.9 fusion.3
  110.1 0.9 fusion.11
  111.1 0.9 fusion.19
  112.0 0.9 fusion.27
  (87 shorter events, 14.3 us)
Async XLA Ops:
  7.2 50.9 %all-gather.4.cloned.1.call-start = ((), (), s32[]{:S(2)}) async-start(), calls=%async_computation | async-start | bytes 4718592 | tf_op jit(solution)/shard_map/all_gather | solution.py:67
  8.0 3.2 %collective-permute-start = (f32[8,128]{1,0:T(8,128)S(1)}, f32[8,128]{1,0:T(8,128)S(1)}, u32[]{:S(2)}, u32[]{:S(2)}) collective-permute-start(f32[8,128]{1,0:T(8,128)S(1)} %slice_bitcast_fusion.12), channel_id=1, source_target_pairs={{0,4},{4,8},{8,12},{12,16},{16,20},{20,24},{24,28},{1,5},{5,9},{9,... | collective-permute-start | bytes 12296 | tf_op jit(solution)/shard_map/ppermute | solution.py:10
  11.9 4.8 %copy-start.2 = (f32[4,8,128,128]{3,2,1,0:T(8,128)S(1)}, f32[4,8,128,128]{3,2,1,0:T(8,128)}, u32[]{:S(2)}) copy-start(f32[4,8,128,128]{3,2,1,0:T(8,128)} %param.6) | copy-start | bytes 6291460
  11.9 5.7 %copy-start.3 = (f32[4,8,128]{2,1,0:T(8,128)S(1)}, f32[4,8,128]{2,1,0:T(8,128)}, u32[]{:S(2)}) copy-start(f32[4,8,128]{2,1,0:T(8,128)} %param.7) | copy-start | bytes 49156
  58.0 6.1 %copy-start = (f32[64,128,128]{2,1,0:T(8,128)S(1)}, f32[64,128,128]{2,1,0:T(8,128)}, u32[]{:S(2)}) copy-start(f32[64,128,128]{2,1,0:T(8,128)} %all-gather.4.cloned.1.call-done) | copy-start | bytes 12582916
  75.4 4.0 %collective-permute-start.1 = (f32[1,8,128]{2,1,0:T(8,128)S(1)}, f32[1,8,128]{2,1,0:T(8,128)S(1)}, u32[]{:S(2)}, u32[]{:S(2)}) collective-permute-start(f32[1,8,128]{2,1,0:T(8,128)S(1)} %multiply_bitcast_fusion), channel_id=1, source_target_pairs={{0,4},{4,8},{8,12},{12,16},{16,20},{20,24},{24,28},{28,0},{1,5},{5... | collective-permute-start | bytes 12296 | tf_op jit(solution)/shard_map/ppermute | solution.py:82
  79.4 3.9 %collective-permute-start.2 = (f32[1,8,128]{2,1,0:T(8,128)S(1)}, f32[1,8,128]{2,1,0:T(8,128)S(1)}, u32[]{:S(2)}, u32[]{:S(2)}) collective-permute-start(f32[1,8,128]{2,1,0:T(8,128)S(1)} %collective-permute-done.1), channel_id=1, source_target_pairs={{0,4},{4,8},{8,12},{12,16},{16,20},{20,24},{24,28},{28,0},{1,5},{5... | collective-permute-start | bytes 12296 | tf_op jit(solution)/shard_map/ppermute | solution.py:82
  83.3 3.9 %collective-permute-start.3 = (f32[1,8,128]{2,1,0:T(8,128)S(1)}, f32[1,8,128]{2,1,0:T(8,128)S(1)}, u32[]{:S(2)}, u32[]{:S(2)}) collective-permute-start(f32[1,8,128]{2,1,0:T(8,128)S(1)} %collective-permute-done.2), channel_id=1, source_target_pairs={{0,4},{4,8},{8,12},{12,16},{16,20},{20,24},{24,28},{28,0},{1,5},{5... | collective-permute-start | bytes 12296 | tf_op jit(solution)/shard_map/ppermute | solution.py:82
  87.2 3.9 %collective-permute-start.4 = (f32[1,8,128]{2,1,0:T(8,128)S(1)}, f32[1,8,128]{2,1,0:T(8,128)S(1)}, u32[]{:S(2)}, u32[]{:S(2)}) collective-permute-start(f32[1,8,128]{2,1,0:T(8,128)S(1)} %collective-permute-done.3), channel_id=1, source_target_pairs={{0,4},{4,8},{8,12},{12,16},{16,20},{20,24},{24,28},{28,0},{1,5},{5... | collective-permute-start | bytes 12296 | tf_op jit(solution)/shard_map/ppermute | solution.py:82
  91.2 3.9 %collective-permute-start.5 = (f32[1,8,128]{2,1,0:T(8,128)S(1)}, f32[1,8,128]{2,1,0:T(8,128)S(1)}, u32[]{:S(2)}, u32[]{:S(2)}) collective-permute-start(f32[1,8,128]{2,1,0:T(8,128)S(1)} %collective-permute-done.4), channel_id=1, source_target_pairs={{0,4},{4,8},{8,12},{12,16},{16,20},{20,24},{24,28},{28,0},{1,5},{5... | collective-permute-start | bytes 12296 | tf_op jit(solution)/shard_map/ppermute | solution.py:82
  95.1 3.9 %collective-permute-start.6 = (f32[1,8,128]{2,1,0:T(8,128)S(1)}, f32[1,8,128]{2,1,0:T(8,128)S(1)}, u32[]{:S(2)}, u32[]{:S(2)}) collective-permute-start(f32[1,8,128]{2,1,0:T(8,128)S(1)} %collective-permute-done.5), channel_id=1, source_target_pairs={{0,4},{4,8},{8,12},{12,16},{16,20},{20,24},{24,28},{28,0},{1,5},{5... | collective-permute-start | bytes 12296 | tf_op jit(solution)/shard_map/ppermute | solution.py:82
  95.1 11.2 %copy-start.1 = (f32[64,128,128]{2,1,0:T(8,128)S(1)}, f32[64,128,128]{2,1,0:T(8,128)}, u32[]{:S(2)}) copy-start(f32[64,128,128]{2,1,0:T(8,128)} %all-gather.4.cloned.1.call-done) | copy-start | bytes 12582916
  99.0 3.9 %collective-permute-start.7 = (f32[1,8,128]{2,1,0:T(8,128)S(1)}, f32[1,8,128]{2,1,0:T(8,128)S(1)}, u32[]{:S(2)}, u32[]{:S(2)}) collective-permute-start(f32[1,8,128]{2,1,0:T(8,128)S(1)} %collective-permute-done.6), channel_id=1, source_target_pairs={{0,4},{4,8},{8,12},{12,16},{16,20},{20,24},{24,28},{28,0},{1,5},{5... | collective-permute-start | bytes 12296 | tf_op jit(solution)/shard_map/ppermute | solution.py:82
  106.9 6.1 %copy-start.4 = (s32[4,8,128]{2,1,0:T(8,128)S(1)}, s32[4,8,128]{2,1,0:T(8,128)}, u32[]{:S(2)}) copy-start(s32[4,8,128]{2,1,0:T(8,128)} %param.10) | copy-start | bytes 49156
Sparse Core Ops, SparseCore 0:
  16.8 41.1 all-gather.3
